TPU v7x, 32 devices: a whole 2x2x4 slice. The times are simulated.
32 devices in a mesh: integral: 4 (over x, core), pair: 8 (over z, y).
Axes of the slice: x: 2, y: 2, z: 4, core: 2. Of those that a mesh axis runs over, the one named last changes fastest.
Arguments:
- t2_tiles: bfloat16 [1024, 20, 1024], P('pair', None, 'integral'), may hold values from -6 to 6
- keep_tile: int32 [20], replicated, may hold values from 0 to 31, as said below
- integrals: bfloat16 [32, 1024, 4096], P('pair', None, 'integral'), may hold values from -0.078125 to 0.078125
Outputs:
- residual: bfloat16 [1024, 4096], P('pair', 'integral')
Inputs may be any that keep to these rules, and one draw needn't show every extreme that they name: `keep_tile`: 20 distinct tile numbers in no particular order; tile k lies in the integral rows of pair index k // 4; at least one pair index has all 4 of its tiles listed.
All inputs are finite; a program needn't handle non-finite values.
Results may differ from a plain program's by a relative error of at most 0.0014.
Values may be sent and summed in bfloat16 or wider, within the bound.
A program may use at most 128 MiB of HBM per device.

v0:
```python
import functools
import itertools

import jax
import jax.numpy as jnp
from jax import lax
from jax.experimental import pallas as pl
from jax.experimental.pallas import tpu as pltpu
from jax.sharding import PartitionSpec as P

MESH = pl.DeviceIdType.MESH
CORES = 2
HALVES = 2
CUTS = 2


def inner_of(count):
    return 2 ** ((count.bit_length() - 1) // 2)


def order_of(count, first):
    away = sorted((at for at in range(count) if at != first), key=lambda at: -abs(at - first))
    return away + [first]


def ladder_kernel(
    dims, idx_ref, t2_ref, v_ref, out_ref,
    packed, amps, ints, part, y_in, low_in, high_in,
    v_sem, own_sem, a_send, a_recv, x_send, x_recv, c_send, c_recv, y_send, y_recv, z_send, low_recv, high_recv,
):
    np_, ny, ni, slots, rows, cols = dims
    nz, nx = np_ // ny, ni // CORES
    piece = rows // CUTS
    kept = t2_ref.shape[0]
    qw = v_ref.shape[2]
    p, i = lax.axis_index("pair"), lax.axis_index("integral")
    z, y = p // ny, p % ny
    x, c = i // CORES, i % CORES
    other = x * CORES + (1 - c)
    tables = [order_of(nz, at) for at in range(nz)]
    order = [sum(jnp.where(z == at, tables[at][k], 0) for at in range(nz)) for k in range(nz)]

    load_v = pltpu.make_async_copy(v_ref, ints, v_sem)
    load_v.start()

    barrier = pltpu.get_barrier_semaphore()
    for d in range(1, np_):
        pl.semaphore_signal(barrier, inc=1, device_id={"pair": (p + d) % np_}, device_id_type=MESH)
    for d in range(1, nx):
        pl.semaphore_signal(
            barrier, inc=1, device_id={"integral": ((x + d) % nx) * CORES + c}, device_id_type=MESH
        )
    pl.semaphore_signal(barrier, inc=1, device_id={"integral": other}, device_id_type=MESH)

    def pack(owner, r):
        for s in range(slots):
            at = idx_ref[owner * slots + s]
            tile = t2_ref[jnp.minimum(at, kept - 1), r * piece : (r + 1) * piece, :]
            packed[owner, r, s] = jnp.where(at < kept, tile, jnp.zeros_like(tile))

    def block(source, r, part_i):
        start = (((source // ny) * CUTS + r) * ny + source % ny) * piece
        return amps.at[:, pl.ds(pl.multiple_of(start, piece), piece), pl.ds(pl.multiple_of(part_i * cols, cols), cols)]

    def a_copy(dest, source, r):
        return pltpu.make_async_remote_copy(
            src_ref=packed.at[dest, r], dst_ref=block(source, r, i),
            send_sem=a_send.at[dest, r], recv_sem=a_recv.at[source, r],
            device_id={"pair": dest}, device_id_type=MESH,
        )

    def x_copy(source, r, dest_x, from_x):
        region = block(source, r, from_x * CORES + c)
        return pltpu.make_async_remote_copy(
            src_ref=region, dst_ref=region, send_sem=x_send.at[dest_x, source, r], recv_sem=x_recv.at[from_x, source, r],
            device_id={"integral": dest_x * CORES + c}, device_id_type=MESH,
        )

    def c_copy(source, r, part_x, part_c):
        region = block(source, r, part_x * CORES + part_c)
        return pltpu.make_async_remote_copy(
            src_ref=region, dst_ref=region, send_sem=c_send.at[part_x, source, r], recv_sem=c_recv.at[part_x, source, r],
            device_id={"integral": other}, device_id_type=MESH,
        )

    def own_copy(r):
        return pltpu.make_async_copy(packed.at[p, r], block(p, r, i), own_sem.at[r])

    def y_copy(zc, r, d, h):
        return pltpu.make_async_remote_copy(
            src_ref=part.at[zc, r, (y + d) % ny, h], dst_ref=y_in.at[d - 1, zc, r, h],
            send_sem=y_send.at[d - 1, zc, r, h], recv_sem=y_recv.at[d - 1, zc, r, h],
            device_id={"pair": z * ny + (y + d) % ny}, device_id_type=MESH,
        )

    def up_copy(zc, r, h):
        return pltpu.make_async_remote_copy(
            src_ref=part.at[zc, r, y, h], dst_ref=low_in.at[zc, r, h],
            send_sem=z_send.at[zc, r, h], recv_sem=low_recv.at[zc, r, h],
            device_id={"pair": (p + ny) % np_}, device_id_type=MESH,
        )

    def down_copy(zc, r, h):
        return pltpu.make_async_remote_copy(
            src_ref=part.at[zc, r, y, h], dst_ref=high_in.at[zc, r, h],
            send_sem=z_send.at[zc, r, h], recv_sem=high_recv.at[zc, r, h],
            device_id={"pair": (p + np_ - ny) % np_}, device_id_type=MESH,
        )

    def send_order():
        for dz, r, dy in itertools.product(range(nz), range(CUTS), range(ny)):
            yield dz, r, dy, order[dz] * ny + (y + dy) % ny

    first = True
    for dz, r, dy, dest in send_order():
        pack(dest, r)
        if dz == nz - 1 and dy == 0:
            own_copy(r).start()
            continue
        if first:
            pl.semaphore_wait(barrier, np_ - 1 + nx - 1 + 1)
            first = False
        a_copy(dest, p, r).start()

    def sources(k):
        zc = order[k]
        for dy in range(ny):
            yield dy, zc * ny + (y + ny - dy) % ny

    def spread(k, r):
        for dy, source in sources(k):
            if k == nz - 1 and dy == 0:
                own_copy(r).wait()
            else:
                a_copy(p, source, r).wait_recv()
            for d in range(1, nx):
                x_copy(source, r, (x + d) % nx, x).start()
            c_copy(source, r, x, c).start()

    def forward(k, r):
        for dy, source in sources(k):
            for d in range(1, nx):
                from_x = (x + d) % nx
                x_copy(source, r, x, from_x).wait_recv()
                c_copy(source, r, from_x, c).start()

    def multiply(k, r):
        zc = order[k]
        for dy, source in sources(k):
            for xx in range(nx):
                c_copy(source, r, xx, 1 - c).wait_recv()
        if k == 0 and r == 0:
            load_v.wait()
        span = ny * piece
        left = pl.ds(pl.multiple_of((zc * CUTS + r) * span, span), span)
        wide = 512
        part_cols = qw // HALVES
        for h in range(HALVES):
            @pl.loop(0, part_cols // wide)
            def _(n):
                right = pl.ds(pl.multiple_of(h * part_cols + n * wide, wide), wide)
                into = pl.ds(pl.multiple_of(n * wide, wide), wide)
                total = jnp.zeros((span, wide), jnp.float32)
                for s in range(slots):
                    total += jnp.dot(amps[s, left, :], ints[s, :, right], preferred_element_type=jnp.float32)
                part[zc, r, :, h, :, into] = total.reshape(ny, piece, wide)

            for d in range(1, ny):
                y_copy(zc, r, d, h).start()

    def reduce_y(k, r):
        zc = order[k]
        for h in range(HALVES):
            for d in range(1, ny):
                y_copy(zc, r, d, h).wait_recv()
            total = part[zc, r, y, h]
            for d in range(1, ny):
                total += y_in[d - 1, zc, r, h]
            part[zc, r, y, h] = total
            if k < nz - 1:
                @pl.when((z == 0) & (zc > z))
                def _():
                    up_copy(zc, r, h).start()

                @pl.when((z == nz - 1) & (zc < z))
                def _():
                    down_copy(zc, r, h).start()

    def reduce_z(k, r):
        zc = order[k]
        for h in range(HALVES):
            @pl.when((z > 0) & (zc > z))
            def _():
                up_copy(zc, r, h).wait_recv()
                part[zc, r, y, h] += low_in[zc, r, h]
                up_copy(zc, r, h).start()

            @pl.when((z < nz - 1) & (zc < z))
            def _():
                down_copy(zc, r, h).wait_recv()
                part[zc, r, y, h] += high_in[zc, r, h]
                down_copy(zc, r, h).start()

    steps = list(itertools.product(range(nz), range(CUTS)))
    for t in range(len(steps) + 3):
        if t < len(steps):
            spread(*steps[t])
        if 0 <= t - 1 < len(steps):
            forward(*steps[t - 1])
            multiply(*steps[t - 1])
        if 0 <= t - 2 < len(steps):
            reduce_y(*steps[t - 2])
        if 0 <= t - 3 < len(steps) - CUTS:
            reduce_z(*steps[t - 3])

    width = qw // HALVES
    for r, h in itertools.product(range(CUTS), range(HALVES)):
        @pl.when(z > 0)
        def _():
            up_copy(z, r, h).wait_recv()
            part[z, r, y, h] += low_in[z, r, h]

        @pl.when(z < nz - 1)
        def _():
            down_copy(z, r, h).wait_recv()
            part[z, r, y, h] += high_in[z, r, h]

        out_ref[r * piece : (r + 1) * piece, h * width : (h + 1) * width] = (0.5 * part[z, r, y, h]).astype(out_ref.dtype)

    for dz, r, dy, dest in send_order():
        if dz < nz - 1 or dy:
            a_copy(dest, p, r).wait_send()
    for k, r in steps:
        zc = order[k]
        for dy, source in sources(k):
            for d in range(1, nx):
                x_copy(source, r, (x + d) % nx, x).wait_send()
            for xx in range(nx):
                c_copy(source, r, xx, c).wait_send()
        for h in range(HALVES):
            for d in range(1, ny):
                y_copy(zc, r, d, h).wait_send()
            if k < nz - 1:
                up_copy(zc, r, h).wait_send()


def on_device(t2_tiles, keep_tile, integrals):
    np_, ni = lax.axis_size("pair"), lax.axis_size("integral")
    rows, kept, cols = t2_tiles.shape
    slots, tt, qw = integrals.shape
    ny = inner_of(np_)
    nz, nx = np_ // ny, ni // CORES
    tiles = jnp.arange(np_ * slots, dtype=jnp.int32)
    positions = jnp.arange(kept, dtype=jnp.int32)
    idx = kept + jnp.sum(jnp.where(keep_tile[None, :] == tiles[:, None], positions[None, :] - kept, 0), axis=1)
    by_tile = jnp.swapaxes(t2_tiles, 0, 1)
    dma = pltpu.SemaphoreType.DMA
    piece = rows // CUTS
    dims = (np_, ny, ni, slots, rows, cols)
    return pl.pallas_call(
        functools.partial(ladder_kernel, dims),
        out_shape=jax.ShapeDtypeStruct((rows, qw), jnp.bfloat16),
        in_specs=[
            pl.BlockSpec(memory_space=pltpu.SMEM),
            pl.BlockSpec(memory_space=pltpu.VMEM),
            pl.BlockSpec(memory_space=pl.ANY),
        ],
        out_specs=pl.BlockSpec(memory_space=pltpu.VMEM),
        scratch_shapes=[
            pltpu.VMEM((np_, CUTS, slots, piece, cols), jnp.bfloat16),
            pltpu.VMEM((slots, np_ * rows, tt), jnp.bfloat16),
            pltpu.VMEM((slots, tt, qw), jnp.bfloat16),
            pltpu.VMEM((nz, CUTS, ny, HALVES, piece, qw // HALVES), jnp.float32),
            pltpu.VMEM((ny - 1, nz, CUTS, HALVES, piece, qw // HALVES), jnp.float32),
            pltpu.VMEM((nz, CUTS, HALVES, piece, qw // HALVES), jnp.float32),
            pltpu.VMEM((nz, CUTS, HALVES, piece, qw // HALVES), jnp.float32),
            dma, dma((CUTS,)),
            dma((np_, CUTS)), dma((np_, CUTS)),
            dma((nx, np_, CUTS)), dma((nx, np_, CUTS)),
            dma((nx, np_, CUTS)), dma((nx, np_, CUTS)),
            dma((ny - 1, nz, CUTS, HALVES)), dma((ny - 1, nz, CUTS, HALVES)),
            dma((nz, CUTS, HALVES)), dma((nz, CUTS, HALVES)), dma((nz, CUTS, HALVES)),
        ],
        compiler_params=pltpu.CompilerParams(
            collective_id=0, has_side_effects=True, vmem_limit_bytes=60 * 1024 * 1024
        ),
    )(idx.astype(jnp.int32), by_tile, integrals)


def solution(mesh):
    placed = (P("pair", None, "integral"), P(), P("pair", None, "integral"))
    return jax.shard_map(
        on_device, mesh=mesh, in_specs=placed, out_specs=P("pair", "integral"), check_vma=False
    )
```

profile of v0, /device:TPU:24, one launch (start us, length us, event | category | flops | bytes accessed | tf_op | source)
XLA Modules:
  0.0 98.8 jit_solution(14506709097611860371)
XLA Ops:
  0.0 0.7 select_reduce_fusion
  0.7 0.5 broadcast_add_fusion.idx_ref
  1.3 95.9 %shard_map.37 = bf16[128,1024]{1,0:T(8,128)(2,1)} custom-call(s32[32]{0:T(128)} %broadcast_add_fusion.idx_ref, bf16[20,128,256]{2,1,0:T(8,128)(2,1)} %bitcast.1, bf16[4,1024,1024]{2,1,0:T(8,128)(2,1)} %v_ref.1), custom_call_target="tpu_custom_call" | custom-call | tf_op jit(solution)/shard_map/pallas_call | solution.py:260
  97.2 1.7 %copy.5 = bf16[128,1024]{1,0:T(8,128)(2,1)} copy(bf16[128,1024]{1,0:T(8,128)(2,1)} %shard_map.37) | data formatting | bytes 524288
  (1 shorter events, 0.0 us)
where the time goes:
time: 99 us; the launch traced here: 98.8 us
  Pallas kernels  95.9 us (97%)
  local copies, waits for them, and re-layouts  1.67 us (2%)
  other arithmetic  1.26 us (1%)
    pallas_call x1, Pallas kernels, on_device(): pl.pallas_call(functools.partial(ladder_kernel, dims), out_shape=jax.Shap...  95.9 us

commit v1 on v0

v1 whole, which is shorter than its diff:
```python
import functools
import itertools

import jax
import jax.numpy as jnp
from jax import lax
from jax.experimental import pallas as pl
from jax.experimental.pallas import tpu as pltpu
from jax.sharding import PartitionSpec as P

MESH = pl.DeviceIdType.MESH
CORES = 2
HALVES = 2
CUTS = 2
AHEAD = ((-1, -1), (-1, -1), (-1, 1), (3, 4))
LAG = 2
LANES = 128
SUB = 8
LEVELS = 32766.0
TINY = 2e-34


def inner_of(count):
    return 2 ** ((count.bit_length() - 1) // 2)


def plan_of(count, cuts):
    steps = count * cuts
    if count & (count - 1):
        order = [[(k - z) % count for k in range(2 * z, 2 * z + count)] for z in range(count)]
    else:
        order = [[z ^ k ^ (k >> 1) for k in range(count)] for z in range(count)]
    late = {}
    for zc in range(count):
        for zs in (range(zc), range(count - 1, zc, -1)):
            before = None
            for z in zs:
                for r in range(cuts):
                    ready = order[z].index(zc) * cuts + r + 2
                    late[z, zc, r] = ready if before is None else max(ready, late[before, zc, r] + LAG)
                before = z
    last = max(late.values())
    passes = [[[[] for _ in range(count)] for _ in range(cuts)] for _ in range(last + 1)]
    for (z, zc, r), at in late.items():
        if 0 < z < count - 1:
            passes[at][r][z].append(zc)
    return order, passes, max(last + 1, steps + 2)


def release(k, r):
    return AHEAD[k][r] if k < len(AHEAD) else AHEAD[-1][r] + (k + 1 - len(AHEAD)) * CUTS


def ladder_kernel(
    dims, keep_ref, t2_ref, v_ref, out_ref,
    tiles, packed, amps, ints, part, y_out, y_scale, y_in, y_in_scale, z_out, z_scale, z_in, z_in_scale,
    v_sem, t_sem, own_sem, a_send, a_recv, x_send, x_recv, c_send, c_recv, y_send, y_recv, z_send, z_recv,
):
    np_, ny, ni, slots, rows, cols = dims
    nz, nx = np_ // ny, ni // CORES
    piece = rows // CUTS
    kept = t2_ref.shape[0]
    qw = v_ref.shape[2]
    width = qw // HALVES
    p, i = lax.axis_index("pair"), lax.axis_index("integral")
    z, y = p // ny, p % ny
    x, c = i // CORES, i % CORES
    other = x * CORES + (1 - c)
    tables, passes, loops = plan_of(nz, CUTS)

    def pick(values):
        return sum(jnp.where(z == at, values[at], 0) for at in range(nz))

    order = [pick([tables[at][k] for at in range(nz)]) for k in range(nz)]

    load_t = pltpu.make_async_copy(t2_ref, tiles, t_sem)
    load_t.start()
    load_v = pltpu.make_async_copy(v_ref, ints, v_sem)

    barrier = pltpu.get_barrier_semaphore()
    for d in range(1, np_):
        pl.semaphore_signal(barrier, inc=1, device_id={"pair": (p + d) % np_}, device_id_type=MESH)
    for d in range(1, nx):
        pl.semaphore_signal(
            barrier, inc=1, device_id={"integral": ((x + d) % nx) * CORES + c}, device_id_type=MESH
        )
    pl.semaphore_signal(barrier, inc=1, device_id={"integral": other}, device_id_type=MESH)

    def places(owner):
        found = []
        for s in range(slots):
            tile = owner * slots + s
            at = jnp.int32(kept)
            for j in range(kept):
                at = jnp.where(keep_ref[j] == tile, j, at)
            found.append(at)
        return found

    def pack(owner, r, found):
        for s in range(slots):
            tile = tiles[jnp.minimum(found[s], kept - 1), r * piece : (r + 1) * piece, :]
            packed[owner, r, s] = jnp.where(found[s] < kept, tile, jnp.zeros_like(tile))

    def block(source, r, part_i):
        start = (((source // ny) * CUTS + r) * ny + source % ny) * piece
        return amps.at[:, pl.ds(pl.multiple_of(start, piece), piece), pl.ds(pl.multiple_of(part_i * cols, cols), cols)]

    def a_copy(dest, source, r):
        return pltpu.make_async_remote_copy(
            src_ref=packed.at[dest, r], dst_ref=block(source, r, i),
            send_sem=a_send.at[dest, r], recv_sem=a_recv.at[source, r],
            device_id={"pair": dest}, device_id_type=MESH,
        )

    def x_copy(source, r, dest_x, from_x):
        region = block(source, r, from_x * CORES + c)
        return pltpu.make_async_remote_copy(
            src_ref=region, dst_ref=region, send_sem=x_send.at[dest_x, source, r], recv_sem=x_recv.at[from_x, source, r],
            device_id={"integral": dest_x * CORES + c}, device_id_type=MESH,
        )

    def c_copy(source, r, part_x, part_c):
        region = block(source, r, part_x * CORES + part_c)
        return pltpu.make_async_remote_copy(
            src_ref=region, dst_ref=region, send_sem=c_send.at[part_x, source, r], recv_sem=c_recv.at[part_x, source, r],
            device_id={"integral": other}, device_id_type=MESH,
        )

    def own_copy(r):
        return pltpu.make_async_copy(packed.at[p, r], block(p, r, i), own_sem.at[r])

    def y_copies(zc, r, d, h):
        pairs = ((y_out, y_in), (y_scale, y_in_scale))
        return [
            pltpu.make_async_remote_copy(
                src_ref=src.at[d - 1, zc, r, h], dst_ref=dst.at[d - 1, zc, r, h],
                send_sem=y_send.at[n, d - 1, zc, r, h], recv_sem=y_recv.at[n, d - 1, zc, r, h],
                device_id={"pair": z * ny + (y + d) % ny}, device_id_type=MESH,
            )
            for n, (src, dst) in enumerate(pairs)
        ]

    def z_copies(zc, slot, r, h):
        to = jnp.where(zc > z, p + ny, p + np_ - ny) % np_
        pairs = ((z_out, z_in), (z_scale, z_in_scale))
        return [
            pltpu.make_async_remote_copy(
                src_ref=src.at[zc, r, h], dst_ref=dst.at[slot, r, h],
                send_sem=z_send.at[n, zc, r, h], recv_sem=z_recv.at[n, slot, r, h],
                device_id={"pair": to}, device_id_type=MESH,
            )
            for n, (src, dst) in enumerate(pairs)
        ]

    def z_slot(zc):
        return jnp.where(zc == z - 1, nz, zc)

    def lanes_of(g):
        return pl.ds(pl.multiple_of(g * LANES, LANES), LANES)

    def absorb(total, code, scale):
        step = scale[...]

        @pl.loop(0, width // LANES)
        def _(g):
            at = lanes_of(g)
            gain = code[:, at].astype(jnp.float32).reshape(piece // SUB, SUB, LANES) * step[None]
            total[:, at] += gain.reshape(piece, LANES)

    def encode(total, code, scale):
        def most(g, top):
            values = jnp.abs(total[:, lanes_of(g)]).reshape(piece // SUB, SUB, LANES)
            return jnp.maximum(top, jnp.max(values, axis=0))

        top = lax.fori_loop(0, width // LANES, most, jnp.full((SUB, LANES), TINY, jnp.float32))
        scale[...] = top * (1.0 / LEVELS)
        gain = LEVELS / top

        @pl.loop(0, width // LANES)
        def _(g):
            at = lanes_of(g)
            values = total[:, at].reshape(piece // SUB, SUB, LANES) * gain[None]
            code[:, at] = jnp.round(values).reshape(piece, LANES).astype(jnp.int32).astype(jnp.int16)

    load_t.wait()
    load_v.start()
    own_places = places(p)
    for r in range(CUTS):
        pack(p, r, own_places)
        own_copy(r).start()
    pl.semaphore_wait(barrier, np_ - 1 + nx - 1 + 1)

    def send_rows(k, r):
        plane = order[k]
        for dy in range(ny):
            dest = plane * ny + (y + dy) % ny
            if k or dy:
                if r == 0:
                    found[k, dy] = places(dest)
                    for each in range(CUTS):
                        pack(dest, each, found[k, dy])
                a_copy(dest, p, r).start()

    found = {}

    def sources(k):
        zc = order[k]
        for dy in range(ny):
            yield dy, zc * ny + (y + ny - dy) % ny

    def spread_one(source, r):
        for d in range(1, nx):
            x_copy(source, r, (x + d) % nx, x).start()
        c_copy(source, r, x, c).start()

    def spread(k, r):
        for dy, source in sources(k):
            if k or dy:
                a_copy(p, source, r).wait_recv()
                spread_one(source, r)

    def first():
        for r in range(CUTS):
            own_copy(r).wait()
            spread_one(p, r)
            for k in range(nz):
                if release(k, r) < 0:
                    send_rows(k, r)

    def forward(k, r):
        for dy, source in sources(k):
            for d in range(1, nx):
                from_x = (x + d) % nx
                x_copy(source, r, x, from_x).wait_recv()
                c_copy(source, r, from_x, c).start()

    def multiply(k, r):
        zc = order[k]
        for dy, source in sources(k):
            for xx in range(nx):
                c_copy(source, r, xx, 1 - c).wait_recv()
        if k == 0 and r == 0:
            load_v.wait()
        span = ny * piece
        left = pl.ds(pl.multiple_of((zc * CUTS + r) * span, span), span)
        wide = min(512, width)
        for h in range(HALVES):
            @pl.loop(0, width // wide)
            def _(n):
                right = pl.ds(pl.multiple_of(h * width + n * wide, wide), wide)
                into = pl.ds(pl.multiple_of(n * wide, wide), wide)
                total = jnp.zeros((span, wide), jnp.float32)
                for s in range(slots):
                    total += jnp.dot(amps[s, left, :], ints[s, :, right], preferred_element_type=jnp.float32)
                part[zc, r, h, :, :, into] = total.reshape(ny, piece, wide)

            for d in range(1, ny):
                encode(part.at[zc, r, h, (y + d) % ny], y_out.at[d - 1, zc, r, h], y_scale.at[d - 1, zc, r, h])
                for copy in y_copies(zc, r, d, h):
                    copy.start()

    def hand_on(zc, r, h):
        encode(part.at[zc, r, h, y], z_out.at[zc, r, h], z_scale.at[zc, r, h])
        for copy in z_copies(zc, z_slot(zc), r, h):
            copy.start()

    def take(slot, zc, r, h):
        for copy in z_copies(zc, slot, r, h):
            copy.wait_recv()
        absorb(part.at[zc, r, h, y], z_in.at[slot, r, h], z_in_scale.at[slot, r, h])

    def reduce_y(k, r):
        zc = order[k]
        for h in range(HALVES):
            for d in range(1, ny):
                for copy in y_copies(zc, r, d, h):
                    copy.wait_recv()
                absorb(part.at[zc, r, h, y], y_in.at[d - 1, zc, r, h], y_in_scale.at[d - 1, zc, r, h])
            if k > 0:
                @pl.when((z == 0) | (z == nz - 1))
                def _():
                    hand_on(zc, r, h)

    def pass_on(at):
        for r in range(CUTS):
            now = passes[at][r]
            for n in range(max(len(some) for some in now)):
                to = [some[n] if n < len(some) else -1 for some in now]
                zc = pick([max(each, 0) for each in to])

                @pl.when(pick([int(each >= 0) for each in to]) > 0)
                def _():
                    for h in range(HALVES):
                        take(zc, zc, r, h)
                        hand_on(zc, r, h)

    steps = list(itertools.product(range(nz), range(CUTS)))
    first()
    for t in range(loops):
        if t < len(steps):
            k, r = steps[t]
            for ahead in steps:
                if release(*ahead) == t:
                    send_rows(*ahead)
            spread(k, r)
        if 0 <= t - 1 < len(steps):
            forward(*steps[t - 1])
            multiply(*steps[t - 1])
        if 0 <= t - 2 < len(steps):
            reduce_y(*steps[t - 2])
        if t < len(passes):
            pass_on(t)

    for r, h in itertools.product(range(CUTS), range(HALVES)):
        @pl.when(z > 0)
        def _():
            take(z, z, r, h)

        @pl.when(z < nz - 1)
        def _():
            take(nz, z, r, h)

        out_ref[r * piece : (r + 1) * piece, h * width : (h + 1) * width] = (0.5 * part[z, r, h, y]).astype(out_ref.dtype)

    for k, r, dy in itertools.product(range(nz), range(CUTS), range(ny)):
        if k or dy:
            a_copy(order[k] * ny + (y + dy) % ny, p, r).wait_send()
    for k, r in steps:
        zc = order[k]
        for dy, source in sources(k):
            for d in range(1, nx):
                x_copy(source, r, (x + d) % nx, x).wait_send()
            for xx in range(nx):
                c_copy(source, r, xx, c).wait_send()
        for h in range(HALVES):
            for d in range(1, ny):
                for copy in y_copies(zc, r, d, h):
                    copy.wait_send()
            if k > 0:
                for copy in z_copies(zc, z_slot(zc), r, h):
                    copy.wait_send()


def on_device(t2_tiles, keep_tile, integrals):
    np_, ni = lax.axis_size("pair"), lax.axis_size("integral")
    rows, kept, cols = t2_tiles.shape
    slots, tt, qw = integrals.shape
    ny = inner_of(np_)
    nz, nx = np_ // ny, ni // CORES
    by_tile = jnp.swapaxes(t2_tiles, 0, 1)
    dma = pltpu.SemaphoreType.DMA
    piece, width = rows // CUTS, qw // HALVES
    dims = (np_, ny, ni, slots, rows, cols)
    y_lead, z_lead, in_lead = (ny - 1, nz, CUTS, HALVES), (nz, CUTS, HALVES), (nz + 1, CUTS, HALVES)
    return pl.pallas_call(
        functools.partial(ladder_kernel, dims),
        out_shape=jax.ShapeDtypeStruct((rows, qw), jnp.bfloat16),
        in_specs=[
            pl.BlockSpec(memory_space=pltpu.SMEM),
            pl.BlockSpec(memory_space=pl.ANY),
            pl.BlockSpec(memory_space=pl.ANY),
        ],
        out_specs=pl.BlockSpec(memory_space=pltpu.VMEM),
        scratch_shapes=[
            pltpu.VMEM((kept, rows, cols), jnp.bfloat16),
            pltpu.VMEM((np_, CUTS, slots, piece, cols), jnp.bfloat16),
            pltpu.VMEM((slots, np_ * rows, tt), jnp.bfloat16),
            pltpu.VMEM((slots, tt, qw), jnp.bfloat16),
            pltpu.VMEM((nz, CUTS, HALVES, ny, piece, width), jnp.float32),
            pltpu.VMEM((*y_lead, piece, width), jnp.int16),
            pltpu.VMEM((*y_lead, SUB, LANES), jnp.float32),
            pltpu.VMEM((*y_lead, piece, width), jnp.int16),
            pltpu.VMEM((*y_lead, SUB, LANES), jnp.float32),
            pltpu.VMEM((*z_lead, piece, width), jnp.int16),
            pltpu.VMEM((*z_lead, SUB, LANES), jnp.float32),
            pltpu.VMEM((*in_lead, piece, width), jnp.int16),
            pltpu.VMEM((*in_lead, SUB, LANES), jnp.float32),
            dma, dma, dma((CUTS,)),
            dma((np_, CUTS)), dma((np_, CUTS)),
            dma((nx, np_, CUTS)), dma((nx, np_, CUTS)),
            dma((nx, np_, CUTS)), dma((nx, np_, CUTS)),
            dma((2, *y_lead)), dma((2, *y_lead)),
            dma((2, *z_lead)), dma((2, *in_lead)),
        ],
        compiler_params=pltpu.CompilerParams(
            collective_id=0, has_side_effects=True, vmem_limit_bytes=60 * 1024 * 1024
        ),
    )(keep_tile.astype(jnp.int32), by_tile, integrals)


def solution(mesh):
    placed = (P("pair", None, "integral"), P(), P("pair", None, "integral"))
    return jax.shard_map(
        on_device, mesh=mesh, in_specs=placed, out_specs=P("pair", "integral"), check_vma=False
    )
```

time: 99 us -> 81.7 us (0.83)
  the two profiles are of different devices: /device:TPU:24 before, /device:TPU:0 now
where the time goes in v1:
time: 81.7 us; the launch traced here: 81.5 us
  Pallas kernels  79.8 us (98%)
  local copies, waits for them, and re-layouts  1.67 us (2%)
    pallas_call x1, Pallas kernels, on_device(): pl.pallas_call(functools.partial(ladder_kernel, dims), out_shape=jax.Shap...  79.8 us
    unnamed x1, local copies, waits for them, and re-layouts  1.67 us

profile of v1, /device:TPU:0, one launch (start us, length us, event | category | flops | bytes accessed | tf_op | source)
XLA Modules:
  0.0 81.5 jit_solution(9099439022125377465)
XLA Ops:
  0.0 79.8 %shard_map.37 = bf16[128,1024]{1,0:T(8,128)(2,1)} custom-call(s32[20]{0:T(128)} %keep_ref.1, bf16[20,128,256]{2,1,0:T(8,128)(2,1)} %bitcast.1, bf16[4,1024,1024]{2,1,0:T(8,128)(2,1)} %v_ref.1), custom_call_target="tpu_custom_call" | custom-call | tf_op jit(solution)/shard_map/pallas_call | solution.py:355
  79.8 1.7 %copy.5 = bf16[128,1024]{1,0:T(8,128)(2,1)} copy(bf16[128,1024]{1,0:T(8,128)(2,1)} %shard_map.37) | data formatting | bytes 524288

commit v2 on v1

--- a/solution.py
+++ b/solution.py
@@ -12,6 +12,10 @@
 CORES = 2
 HALVES = 2
 CUTS = 2
+UNROLL = 4
+MUL_LAG = 2
+SUM_LAG = 3
+WIDE = 512
 AHEAD = ((-1, -1), (-1, -1), (-1, 1), (3, 4))
 LAG = 2
 LANES = 128
@@ -36,7 +40,7 @@
             before = None
             for z in zs:
                 for r in range(cuts):
-                    ready = order[z].index(zc) * cuts + r + 2
+                    ready = order[z].index(zc) * cuts + r + SUM_LAG
                     late[z, zc, r] = ready if before is None else max(ready, late[before, zc, r] + LAG)
                 before = z
     last = max(late.values())
@@ -44,7 +48,7 @@
     for (z, zc, r), at in late.items():
         if 0 < z < count - 1:
             passes[at][r][z].append(zc)
-    return order, passes, max(last + 1, steps + 2)
+    return order, passes, max(last + 1, steps + SUM_LAG)
 
 
 def release(k, r):
@@ -53,8 +57,8 @@
 
 def ladder_kernel(
     dims, keep_ref, t2_ref, v_ref, out_ref,
-    tiles, packed, amps, ints, part, y_out, y_scale, y_in, y_in_scale, z_out, z_scale, z_in, z_in_scale,
-    v_sem, t_sem, own_sem, a_send, a_recv, x_send, x_recv, c_send, c_recv, y_send, y_recv, z_send, z_recv,
+    tiles, packed, result, amps, ints, part, y_out, y_scale, y_in, y_in_scale, z_out, z_scale, z_in, z_in_scale,
+    v_sem, t_sem, own_sem, out_sem, a_send, a_recv, x_send, x_recv, c_send, c_recv, y_send, y_recv, z_send, z_recv,
 ):
     np_, ny, ni, slots, rows, cols = dims
     nz, nx = np_ // ny, ni // CORES
@@ -103,26 +107,26 @@
 
     def block(source, r, part_i):
         start = (((source // ny) * CUTS + r) * ny + source % ny) * piece
-        return amps.at[:, pl.ds(pl.multiple_of(start, piece), piece), pl.ds(pl.multiple_of(part_i * cols, cols), cols)]
+        return amps.at[part_i, :, pl.ds(pl.multiple_of(start, piece), piece), :]
 
     def a_copy(dest, source, r):
         return pltpu.make_async_remote_copy(
             src_ref=packed.at[dest, r], dst_ref=block(source, r, i),
-            send_sem=a_send.at[dest, r], recv_sem=a_recv.at[source, r],
+            send_sem=a_send, recv_sem=a_recv.at[source, r],
             device_id={"pair": dest}, device_id_type=MESH,
         )
 
     def x_copy(source, r, dest_x, from_x):
         region = block(source, r, from_x * CORES + c)
         return pltpu.make_async_remote_copy(
-            src_ref=region, dst_ref=region, send_sem=x_send.at[dest_x, source, r], recv_sem=x_recv.at[from_x, source, r],
+            src_ref=region, dst_ref=region, send_sem=x_send, recv_sem=x_recv.at[from_x, source, r],
             device_id={"integral": dest_x * CORES + c}, device_id_type=MESH,
         )
 
     def c_copy(source, r, part_x, part_c):
         region = block(source, r, part_x * CORES + part_c)
         return pltpu.make_async_remote_copy(
-            src_ref=region, dst_ref=region, send_sem=c_send.at[part_x, source, r], recv_sem=c_recv.at[part_x, source, r],
+            src_ref=region, dst_ref=region, send_sem=c_send, recv_sem=c_recv.at[part_x, source, r],
             device_id={"integral": other}, device_id_type=MESH,
         )
 
@@ -134,7 +138,7 @@
         return [
             pltpu.make_async_remote_copy(
                 src_ref=src.at[d - 1, zc, r, h], dst_ref=dst.at[d - 1, zc, r, h],
-                send_sem=y_send.at[n, d - 1, zc, r, h], recv_sem=y_recv.at[n, d - 1, zc, r, h],
+                send_sem=y_send.at[n], recv_sem=y_recv.at[n, d - 1, zc, r, h],
                 device_id={"pair": z * ny + (y + d) % ny}, device_id_type=MESH,
             )
             for n, (src, dst) in enumerate(pairs)
@@ -146,7 +150,7 @@
         return [
             pltpu.make_async_remote_copy(
                 src_ref=src.at[zc, r, h], dst_ref=dst.at[slot, r, h],
-                send_sem=z_send.at[n, zc, r, h], recv_sem=z_recv.at[n, slot, r, h],
+                send_sem=z_send.at[n], recv_sem=z_recv.at[n, slot, r, h],
                 device_id={"pair": to}, device_id_type=MESH,
             )
             for n, (src, dst) in enumerate(pairs)
@@ -161,7 +165,7 @@
     def absorb(total, code, scale):
         step = scale[...]
 
-        @pl.loop(0, width // LANES)
+        @pl.loop(0, width // LANES, unroll=UNROLL)
         def _(g):
             at = lanes_of(g)
             gain = code[:, at].astype(jnp.float32).reshape(piece // SUB, SUB, LANES) * step[None]
@@ -172,11 +176,11 @@
             values = jnp.abs(total[:, lanes_of(g)]).reshape(piece // SUB, SUB, LANES)
             return jnp.maximum(top, jnp.max(values, axis=0))
 
-        top = lax.fori_loop(0, width // LANES, most, jnp.full((SUB, LANES), TINY, jnp.float32))
+        top = lax.fori_loop(0, width // LANES, most, jnp.full((SUB, LANES), TINY, jnp.float32), unroll=UNROLL)
         scale[...] = top * (1.0 / LEVELS)
         gain = LEVELS / top
 
-        @pl.loop(0, width // LANES)
+        @pl.loop(0, width // LANES, unroll=UNROLL)
         def _(g):
             at = lanes_of(g)
             values = total[:, at].reshape(piece // SUB, SUB, LANES) * gain[None]
@@ -243,15 +247,16 @@
             load_v.wait()
         span = ny * piece
         left = pl.ds(pl.multiple_of((zc * CUTS + r) * span, span), span)
-        wide = min(512, width)
+        wide = min(WIDE, width)
         for h in range(HALVES):
             @pl.loop(0, width // wide)
             def _(n):
                 right = pl.ds(pl.multiple_of(h * width + n * wide, wide), wide)
                 into = pl.ds(pl.multiple_of(n * wide, wide), wide)
                 total = jnp.zeros((span, wide), jnp.float32)
-                for s in range(slots):
-                    total += jnp.dot(amps[s, left, :], ints[s, :, right], preferred_element_type=jnp.float32)
+                for s, at in itertools.product(range(slots), range(ni)):
+                    inner = slice(at * cols, (at + 1) * cols)
+                    total += jnp.dot(amps[at, s, left, :], ints[s, inner, right], preferred_element_type=jnp.float32)
                 part[zc, r, h, :, :, into] = total.reshape(ny, piece, wide)
 
             for d in range(1, ny):
@@ -305,11 +310,25 @@
             spread(k, r)
         if 0 <= t - 1 < len(steps):
             forward(*steps[t - 1])
-            multiply(*steps[t - 1])
-        if 0 <= t - 2 < len(steps):
-            reduce_y(*steps[t - 2])
+        if 0 <= t - MUL_LAG < len(steps):
+            multiply(*steps[t - MUL_LAG])
+        if 0 <= t - SUM_LAG < len(steps):
+            reduce_y(*steps[t - SUM_LAG])
         if t < len(passes):
             pass_on(t)
+
+    def sent(ref, sem):
+        pltpu.make_async_copy(ref, ref, sem).wait()
+
+    sent(packed.at[: np_ - 1], a_send)
+    sent(amps.at[: nx - 1], x_send)
+    sent(amps.at[:nx], c_send)
+    sent(y_out, y_send.at[0])
+    sent(y_scale, y_send.at[1])
+
+    def out_copy(r):
+        at = slice(r * piece, (r + 1) * piece)
+        return pltpu.make_async_copy(result.at[at, :], out_ref.at[at, :], out_sem.at[r])
 
     for r, h in itertools.product(range(CUTS), range(HALVES)):
         @pl.when(z > 0)
@@ -320,25 +339,14 @@
         def _():
             take(nz, z, r, h)
 
-        out_ref[r * piece : (r + 1) * piece, h * width : (h + 1) * width] = (0.5 * part[z, r, h, y]).astype(out_ref.dtype)
-
-    for k, r, dy in itertools.product(range(nz), range(CUTS), range(ny)):
-        if k or dy:
-            a_copy(order[k] * ny + (y + dy) % ny, p, r).wait_send()
-    for k, r in steps:
-        zc = order[k]
-        for dy, source in sources(k):
-            for d in range(1, nx):
-                x_copy(source, r, (x + d) % nx, x).wait_send()
-            for xx in range(nx):
-                c_copy(source, r, xx, c).wait_send()
-        for h in range(HALVES):
-            for d in range(1, ny):
-                for copy in y_copies(zc, r, d, h):
-                    copy.wait_send()
-            if k > 0:
-                for copy in z_copies(zc, z_slot(zc), r, h):
-                    copy.wait_send()
+        result[r * piece : (r + 1) * piece, h * width : (h + 1) * width] = (0.5 * part[z, r, h, y]).astype(result.dtype)
+        if h == HALVES - 1:
+            out_copy(r).start()
+
+    sent(z_out.at[: nz - 1], z_send.at[0])
+    sent(z_scale.at[: nz - 1], z_send.at[1])
+    for r in range(CUTS):
+        out_copy(r).wait()
 
 
 def on_device(t2_tiles, keep_tile, integrals):
@@ -360,11 +368,12 @@
             pl.BlockSpec(memory_space=pl.ANY),
             pl.BlockSpec(memory_space=pl.ANY),
         ],
-        out_specs=pl.BlockSpec(memory_space=pltpu.VMEM),
+        out_specs=pl.BlockSpec(memory_space=pl.ANY),
         scratch_shapes=[
             pltpu.VMEM((kept, rows, cols), jnp.bfloat16),
             pltpu.VMEM((np_, CUTS, slots, piece, cols), jnp.bfloat16),
-            pltpu.VMEM((slots, np_ * rows, tt), jnp.bfloat16),
+            pltpu.VMEM((rows, qw), jnp.bfloat16),
+            pltpu.VMEM((ni, slots, np_ * rows, cols), jnp.bfloat16),
             pltpu.VMEM((slots, tt, qw), jnp.bfloat16),
             pltpu.VMEM((nz, CUTS, HALVES, ny, piece, width), jnp.float32),
             pltpu.VMEM((*y_lead, piece, width), jnp.int16),
@@ -375,12 +384,12 @@
             pltpu.VMEM((*z_lead, SUB, LANES), jnp.float32),
             pltpu.VMEM((*in_lead, piece, width), jnp.int16),
             pltpu.VMEM((*in_lead, SUB, LANES), jnp.float32),
-            dma, dma, dma((CUTS,)),
-            dma((np_, CUTS)), dma((np_, CUTS)),
-            dma((nx, np_, CUTS)), dma((nx, np_, CUTS)),
-            dma((nx, np_, CUTS)), dma((nx, np_, CUTS)),
-            dma((2, *y_lead)), dma((2, *y_lead)),
-            dma((2, *z_lead)), dma((2, *in_lead)),
+            dma, dma, dma((CUTS,)), dma((CUTS,)),
+            dma, dma((np_, CUTS)),
+            dma, dma((nx, np_, CUTS)),
+            dma, dma((nx, np_, CUTS)),
+            dma((2,)), dma((2, *y_lead)),
+            dma((2,)), dma((2, *in_lead)),
         ],
         compiler_params=pltpu.CompilerParams(
             collective_id=0, has_side_effects=True, vmem_limit_bytes=60 * 1024 * 1024

time: 81.7 us -> 78.5 us (0.961)
  Pallas kernels: 79.8 us -> 76.6 us
    pallas_call x1, Pallas kernels: 79.8 us -> 76.6 us  [on_device(): pl.pallas_call(functools.partial(ladder_kernel, dims), out_shape=jax.Shap...]
where the time goes in v2:
time: 78.5 us; the launch traced here: 78.3 us
  Pallas kernels  76.6 us (98%)
  local copies, waits for them, and re-layouts  1.67 us (2%)
    pallas_call x1, Pallas kernels, on_device(): pl.pallas_call(functools.partial(ladder_kernel, dims), out_shape=jax.Shap...  76.6 us
    unnamed x1, local copies, waits for them, and re-layouts  1.67 us

profile of v2, /device:TPU:0, one launch (start us, length us, event | category | flops | bytes accessed | tf_op | source)
XLA Modules:
  0.0 78.3 jit_solution(1458460071520721894)
XLA Ops:
  0.0 76.6 %shard_map.37 = bf16[128,1024]{1,0:T(8,128)(2,1)} custom-call(s32[20]{0:T(128)} %keep_ref.1, bf16[20,128,256]{2,1,0:T(8,128)(2,1)} %bitcast.1, bf16[4,1024,1024]{2,1,0:T(8,128)(2,1)} %v_ref.1), custom_call_target="tpu_custom_call" | custom-call | tf_op jit(solution)/shard_map/pallas_call | solution.py:363
  76.6 1.7 %copy.5 = bf16[128,1024]{1,0:T(8,128)(2,1)} copy(bf16[128,1024]{1,0:T(8,128)(2,1)} %shard_map.37) | data formatting | bytes 524288

commit v3 on v2

--- a/solution.py
+++ b/solution.py
@@ -287,7 +287,7 @@
                     hand_on(zc, r, h)
 
     def pass_on(at):
-        for r in range(CUTS):
+        for r in range(CUTS if at < len(passes) else 0):
             now = passes[at][r]
             for n in range(max(len(some) for some in now)):
                 to = [some[n] if n < len(some) else -1 for some in now]
@@ -301,21 +301,44 @@
 
     steps = list(itertools.product(range(nz), range(CUTS)))
     first()
-    for t in range(loops):
-        if t < len(steps):
-            k, r = steps[t]
-            for ahead in steps:
-                if release(*ahead) == t:
-                    send_rows(*ahead)
-            spread(k, r)
-        if 0 <= t - 1 < len(steps):
+    last = len(steps) - 1
+    early = nz > 2 and tables[0].index(1) * CUTS + CUTS - 1 + SUM_LAG <= last
+
+    def take_early():
+        for r, h in itertools.product(range(CUTS), range(HALVES)):
+            pl.when(z == 1)(functools.partial(take, z, z, r, h))
+            pl.when(z == nz - 2)(functools.partial(take, nz, z, r, h))
+
+    for t in range(last):
+        for ahead in steps:
+            if release(*ahead) == t:
+                send_rows(*ahead)
+        spread(*steps[t])
+        if t >= 1:
             forward(*steps[t - 1])
-        if 0 <= t - MUL_LAG < len(steps):
+        if t >= MUL_LAG:
             multiply(*steps[t - MUL_LAG])
-        if 0 <= t - SUM_LAG < len(steps):
+        if t >= SUM_LAG:
             reduce_y(*steps[t - SUM_LAG])
         if t < len(passes):
             pass_on(t)
+    spread(*steps[last])
+    forward(*steps[last - 1])
+    multiply(*steps[last - 2])
+    multiply(*steps[last - 1])
+    reduce_y(*steps[last - 3])
+    pass_on(last)
+    if early:
+        take_early()
+    forward(*steps[last])
+    reduce_y(*steps[last - 2])
+    pass_on(last + 1)
+    multiply(*steps[last])
+    reduce_y(*steps[last - 1])
+    pass_on(last + 2)
+    reduce_y(*steps[last])
+    for t in range(last + 3, len(passes)):
+        pass_on(t)
 
     def sent(ref, sem):
         pltpu.make_async_copy(ref, ref, sem).wait()
@@ -331,11 +354,11 @@
         return pltpu.make_async_copy(result.at[at, :], out_ref.at[at, :], out_sem.at[r])
 
     for r, h in itertools.product(range(CUTS), range(HALVES)):
-        @pl.when(z > 0)
+        @pl.when(z > int(early))
         def _():
             take(z, z, r, h)
 
-        @pl.when(z < nz - 1)
+        @pl.when(z < nz - 1 - int(early))
         def _():
             take(nz, z, r, h)
 

time: 78.5 us -> 77.5 us (0.987)
  Pallas kernels: 76.6 us -> 75.7 us
    pallas_call x1, Pallas kernels: 76.6 us -> 75.7 us  [on_device(): pl.pallas_call(functools.partial(ladder_kernel, dims), out_shape=jax.Shap...]
where the time goes in v3:
time: 77.5 us; the launch traced here: 77.3 us
  Pallas kernels  75.7 us (98%)
  local copies, waits for them, and re-layouts  1.67 us (2%)
    pallas_call x1, Pallas kernels, on_device(): pl.pallas_call(functools.partial(ladder_kernel, dims), out_shape=jax.Shap...  75.7 us
    unnamed x1, local copies, waits for them, and re-layouts  1.67 us

profile of v3, /device:TPU:0, one launch (start us, length us, event | category | flops | bytes accessed | tf_op | source)
XLA Modules:
  0.0 77.3 jit_solution(10746658587985522497)
XLA Ops:
  0.0 75.7 %shard_map.37 = bf16[128,1024]{1,0:T(8,128)(2,1)} custom-call(s32[20]{0:T(128)} %keep_ref.1, bf16[20,128,256]{2,1,0:T(8,128)(2,1)} %bitcast.1, bf16[4,1024,1024]{2,1,0:T(8,128)(2,1)} %v_ref.1), custom_call_target="tpu_custom_call" | custom-call | tf_op jit(solution)/shard_map/pallas_call | solution.py:386
  75.7 1.7 %copy.5 = bf16[128,1024]{1,0:T(8,128)(2,1)} copy(bf16[128,1024]{1,0:T(8,128)(2,1)} %shard_map.37) | data formatting | bytes 524288

commit v4 on v3

--- a/solution.py
+++ b/solution.py
@@ -118,8 +118,9 @@
 
     def x_copy(source, r, dest_x, from_x):
         region = block(source, r, from_x * CORES + c)
+        away = (dest_x - from_x + nx) % nx - 1
         return pltpu.make_async_remote_copy(
-            src_ref=region, dst_ref=region, send_sem=x_send, recv_sem=x_recv.at[from_x, source, r],
+            src_ref=region, dst_ref=region, send_sem=x_send, recv_sem=x_recv.at[away, source, r],
             device_id={"integral": dest_x * CORES + c}, device_id_type=MESH,
         )
 
@@ -409,7 +410,7 @@
             pltpu.VMEM((*in_lead, SUB, LANES), jnp.float32),
             dma, dma, dma((CUTS,)), dma((CUTS,)),
             dma, dma((np_, CUTS)),
-            dma, dma((nx, np_, CUTS)),
+            dma, dma((nx - 1, np_, CUTS)),
             dma, dma((nx, np_, CUTS)),
             dma((2,)), dma((2, *y_lead)),
             dma((2,)), dma((2, *in_lead)),

time: 77.5 us -> 77.4 us (level)
  no operation moved by 1% of the time
where the time goes in v4:
time: 77.4 us; the launch traced here: 77.2 us
  Pallas kernels  75.5 us (98%)
  local copies, waits for them, and re-layouts  1.67 us (2%)
    pallas_call x1, Pallas kernels, on_device(): pl.pallas_call(functools.partial(ladder_kernel, dims), out_shape=jax.Shap...  75.5 us
    unnamed x1, local copies, waits for them, and re-layouts  1.67 us

profile of v4, /device:TPU:0, one launch (start us, length us, event | category | flops | bytes accessed | tf_op | source)
XLA Modules:
  0.0 77.2 jit_solution(5846425610670779253)
XLA Ops:
  0.0 75.5 %shard_map.37 = bf16[128,1024]{1,0:T(8,128)(2,1)} custom-call(s32[20]{0:T(128)} %keep_ref.1, bf16[20,128,256]{2,1,0:T(8,128)(2,1)} %bitcast.1, bf16[4,1024,1024]{2,1,0:T(8,128)(2,1)} %v_ref.1), custom_call_target="tpu_custom_call" | custom-call | tf_op jit(solution)/shard_map/pallas_call | solution.py:387
  75.5 1.7 %copy.5 = bf16[128,1024]{1,0:T(8,128)(2,1)} copy(bf16[128,1024]{1,0:T(8,128)(2,1)} %shard_map.37) | data formatting | bytes 524288
